TPU v7x, 32 devices: a whole 2x2x4 slice. The times are simulated.
32 devices in a mesh: pair: 2 (over core), vcol: 16 (over z, y, x).
Axes of the slice: x: 2, y: 2, z: 4, core: 2. Of those that a mesh axis runs over, the one named last changes fastest.
Arguments:
- amplitudes: bfloat16 [1280, 4096], P('pair', 'vcol'), may hold values from -6 to 6
- tile_owner: int32 [32], replicated, may hold values from 0 to 31, each once
- integrals: bfloat16 [4096, 4096], P('pair', 'vcol'), may hold values from -0.125 to 0.125
- screening: int32 [20, 32, 32], P('pair'), may hold values 0 or 1
- occ_energy: float32 [1280], P('pair'), may hold values from -1 to -0.2
- virt_energy: float32 [4096], replicated, may hold values from 0.2 to 1
Outputs:
- residual: bfloat16 [1280, 4096], P('pair', 'vcol')
Inputs may be any that keep to these rules, and one draw needn't show every extreme that they name: `tile_owner`: each of the 32 tiles appears exactly once.
All inputs are finite; a program needn't handle non-finite values. No bound on the sum of `screening` on one device may be relied on, other than what follows from the above.
Results may differ from a plain program's by a relative error of at most 0.0036.
Values may be sent and summed in bfloat16 or wider, within the bound.
A program may use at most 64 MiB of HBM per device.

v0:
```python
import jax
import jax.numpy as jnp
from jax import lax
from jax.sharding import PartitionSpec as P

TILE = 128
PBLK = 64
KT_DEV = 2


def one_hot(indices, length):
    return (indices[:, None] == jnp.arange(length, dtype=jnp.int32)[None, :]).astype(jnp.float32)


def gather_rows(panel):
    return lax.all_gather(panel, "pair", axis=0, tiled=True)


def local(amplitudes, tile_owner, integrals, screening, occ_energy, virt_energy):
    pair_local = amplitudes.shape[0]
    tile_count = tile_owner.shape[0]
    width = KT_DEV * TILE
    block_count = pair_local // PBLK
    column = lax.axis_index("vcol")
    first_slot = column * KT_DEV
    owned_tiles = lax.dynamic_slice_in_dim(tile_owner, first_slot, KT_DEV, 0)
    screen_float = screening.astype(jnp.float32)
    natural_tiles = first_slot + jnp.arange(KT_DEV, dtype=jnp.int32)
    panel = gather_rows(integrals)
    picked = jnp.einsum("bct,jt->bcj", screen_float, one_hot(natural_tiles, tile_count))
    marks_slot = jnp.take(picked, tile_owner, axis=1).astype(jnp.bfloat16)
    panel_slot = jnp.take(panel.reshape(tile_count, TILE, width), tile_owner, axis=0)
    piece_in = lax.all_gather(amplitudes, "vcol", axis=1, tiled=True)
    tiles_in = piece_in.shape[1] // TILE
    left_all = piece_in.reshape(block_count, PBLK, tiles_in * TILE)

    def one_block(operands):
        left_rows, marks = operands
        masked = (
            panel_slot.reshape(tiles_in, TILE, KT_DEV, TILE) * marks[:, None, :, None]
        ).reshape(tiles_in * TILE, width)
        return jnp.dot(left_rows, masked, preferred_element_type=jnp.float32)

    summed = lax.map(one_block, (left_all, marks_slot))
    ladder_local = summed.reshape(pair_local, width).astype(jnp.bfloat16)
    ranks = tile_count // KT_DEV
    rows = pair_local // ranks
    parts = ladder_local.reshape(ranks, rows, KT_DEV, TILE).transpose(0, 2, 1, 3)
    spread = lax.all_to_all(parts, "vcol", 0, 0, tiled=True).reshape(tile_count, rows, TILE)
    by_slot = jnp.take(spread, tile_owner, axis=0).reshape(ranks, KT_DEV, rows, TILE)
    back = lax.all_to_all(by_slot, "vcol", 0, 0, tiled=True)
    ladder_owned = back.transpose(0, 2, 1, 3).reshape(pair_local, width).astype(jnp.float32)
    virt_owned = jnp.dot(
        one_hot(owned_tiles, tile_count),
        virt_energy.reshape(tile_count, TILE),
        precision=lax.Precision.HIGHEST,
    ).reshape(width)
    residual = ladder_owned + (virt_owned[None, :] - occ_energy[:, None]) * amplitudes.astype(
        jnp.float32
    )
    return residual.astype(jnp.bfloat16)


def solution(mesh):
    return jax.shard_map(
        local,
        mesh=mesh,
        in_specs=(P("pair", "vcol"), P(), P("pair", "vcol"), P("pair", None, None), P("pair"), P()),
        out_specs=P("pair", "vcol"),
        check_vma=False,
    )
```

profile of v0, /device:TPU:0, one launch (start us, length us, event | category | flops | bytes accessed | tf_op | source)
XLA Modules:
  0.0 183.6 jit_solution(1509187314705847250)
XLA Ops:
  6.5 0.7 all-gather.5.cloned.1.call-update
  7.3 0.7 all-gather.3.cloned.1.call-update
  8.0 1.2 convolution_bitcast_fusion.1
  9.2 0.1 copy.12
  9.3 0.7 compare_select_fusion
  10.0 0.6 gather_fusion
  10.6 0.7 compare_and_fusion
  11.3 0.1 fusion.8
  11.4 0.1 copy.13
  11.5 10.7 %all-gather.5.cloned.1.call-done = bf16[4096,256]{1,0:T(8,128)(2,1)} async-done(((bf16[2048,256]{1,0:T(8,128)(2,1)}), bf16[4096,256]{1,0:T(8,128)(2,1)}) %all-gather.5.cloned.1.call-update) | async-done | bytes 2097168 | tf_op jit(solution)/shard_map/all_gather | solution.py:16
  22.2 3.7 %gather_fusion.1 = bf16[32,128,256]{2,1,0:T(8,128)(2,1)} fusion(bf16[32,128,256]{2,1,0:T(8,128)(2,1)} %bitcast.56, s32[1024]{0:T(1024)S(1)} %pad_clamp_fusion), kind=kCustom, calls=%fused_computation.1 | custom fusion | bytes 4194432 | tf_op jit(solution)/shard_map/jit(_take)/gather | solution.py:32
  25.9 1.8 %broadcast_select_fusion = bf16[32,128,256]{2,1,0:T(8,128)(2,1)S(1)} fusion(bf16[32,128,256]{2,1,0:T(8,128)(2,1)} %gather_fusion.1, pred[32]{0:T(512)(128)(4,1)S(1)} %compare_and_fusion), kind=kLoop, calls=%fused_computation.12 | loop fusion | flops 1048576 | bytes 4194336 | tf_op jit(solution)/shard_map/jit(_take)/select_n | solution.py:32
  27.7 96.8 %all-gather.3.cloned.1.call-done = bf16[640,4096]{1,0:T(8,128)(2,1)} async-done(((bf16[640,256]{1,0:T(8,128)(2,1)}), bf16[640,4096]{1,0:T(8,128)(2,1)}) %all-gather.3.cloned.1.call-update) | async-done | bytes 5242896 | tf_op jit(solution)/shard_map/all_gather | solution.py:33
  124.5 19.2 %while.10 = (s32[]{:T(128)}, bf16[10,64,256]{2,1,0:T(8,128)(2,1)S(1)}, bf16[10,64,4096]{2,1,0:T(8,128)(2,1)}, bf16[10,32,2]{1,2,0:T(2,128)(2,1)S(1)}, bf16[32,128,256]{2,1,0:T(8,128)(2,1)S(1)}, /*index=5*/s32[]{:T(128)}) while((s32[]{:T(128)}, bf16[10,64,256]{2,1,0:T(8,128)(2,1)S(1)}, bf16[10,64,4096]{2,1,0:T(8,128)(2,1)}, ...), condition=%wide.region_1.2_spmd, body=%wide.region_0.1_spmd.sunk | while | flops 135266304 | bytes 6948553 | solution.py:44
  124.5 0.1 copy.23
  124.6 0.1 mul.40
  124.7 0.1 broadcast_multiply_fusion.2
  124.9 1.5 fusion.24
  126.4 0.1 copy.23
  126.5 0.1 mul.40
  126.7 0.1 broadcast_multiply_fusion.2
  126.8 1.5 fusion.24
  128.4 0.1 copy.23
  128.5 0.1 mul.40
  128.6 0.1 broadcast_multiply_fusion.2
  128.7 1.5 fusion.24
  130.3 0.1 copy.23
  130.4 0.1 mul.40
  130.5 0.1 broadcast_multiply_fusion.2
  130.7 1.5 fusion.24
  132.2 0.1 copy.23
  132.3 0.1 mul.40
  132.4 0.1 broadcast_multiply_fusion.2
  132.6 1.5 fusion.24
  134.1 0.1 copy.23
  134.2 0.1 mul.40
  134.4 0.1 broadcast_multiply_fusion.2
  134.5 1.5 fusion.24
  136.1 0.1 copy.23
  136.2 0.1 mul.40
  136.3 0.1 broadcast_multiply_fusion.2
  136.4 1.5 fusion.24
  138.0 0.1 copy.23
  138.1 0.1 mul.40
  138.2 0.1 broadcast_multiply_fusion.2
  138.4 1.5 fusion.24
  139.9 0.1 copy.23
  140.0 0.1 mul.40
  140.1 0.1 broadcast_multiply_fusion.2
  140.3 1.5 fusion.24
  141.8 0.1 copy.23
  141.9 0.1 mul.40
  142.0 0.1 broadcast_multiply_fusion.2
  142.2 1.5 fusion.24
  143.7 0.8 convert_element_type.33
  144.5 3.8 %all-to-all-start = ((bf16[16,2,40,128]{3,1,2,0:T(2,128)(2,1)}), bf16[16,2,40,128]{3,1,2,0:T(2,128)(2,1)S(1)}, u32[]{:S(2)}, u32[]{:S(2)}) async-start(bf16[16,2,40,128]{3,1,2,0:T(2,128)(2,1)} %bitcast.9), calls=%async_computation | async-start | bytes 655360 | tf_op jit(solution)/shard_map/all_to_all | solution.py:49
  148.4 11.2 %all-to-all-done = bf16[16,2,40,128]{3,1,2,0:T(2,128)(2,1)S(1)} async-done(((bf16[16,2,40,128]{3,1,2,0:T(2,128)(2,1)}), bf16[16,2,40,128]{3,1,2,0:T(2,128)(2,1)S(1)}, u32[]{:S(2)}, u32[]{:S(2)}) %all-to-all-start) | async-done | bytes 327712 | tf_op jit(solution)/shard_map/all_to_all | solution.py:49
  159.7 0.6 gather_fusion.2
  160.4 0.8 broadcast_select_fusion.1
  161.2 3.5 %all-to-all-start.1 = ((bf16[16,2,40,128]{3,2,1,0:T(8,128)(2,1)}), bf16[16,2,40,128]{3,2,1,0:T(8,128)(2,1)S(1)}, u32[]{:S(2)}, u32[]{:S(2)}) async-start(bf16[16,2,40,128]{3,2,1,0:T(8,128)(2,1)} %broadcast_select_fusion.1), calls=%async_computation.1 | async-start | bytes 655360 | tf_op jit(solution)/shard_map/all_to_all | solution.py:51
  164.8 0.2 convolution_bitcast_fusion.2
  165.0 10.4 %all-to-all-done.1 = bf16[16,2,40,128]{3,2,1,0:T(8,128)(2,1)S(1)} async-done(((bf16[16,2,40,128]{3,2,1,0:T(8,128)(2,1)}), bf16[16,2,40,128]{3,2,1,0:T(8,128)(2,1)S(1)}, u32[]{:S(2)}, u32[]{:S(2)}) %all-to-all-start.1) | async-done | bytes 327712 | tf_op jit(solution)/shard_map/all_to_all | solution.py:51
  175.5 0.3 copy.15
  175.9 0.9 fusion.5
  (37 shorter events, 0.5 us)
Async XLA Ops:
  6.5 158.3 %copy-start = (f32[4096]{0:T(1024)S(1)}, f32[4096]{0:T(1024)}, u32[]{:S(2)}) copy-start(f32[4096]{0:T(1024)} %param.13) | copy-start | bytes 49156
  6.5 15.7 %all-gather.5.cloned.1.call-start = ((), (), s32[]{:S(2)}) async-start(), calls=%async_computation.3 | async-start | bytes 3145728 | tf_op jit(solution)/shard_map/all_gather | solution.py:16
  7.3 117.2 %all-gather.3.cloned.1.call-start = ((), (), s32[]{:S(2)}) async-start(), calls=%async_computation.2 | async-start | bytes 5570560 | tf_op jit(solution)/shard_map/all_gather | solution.py:33
  143.7 21.0 %copy-start.3 = (s32[32]{0:T(128)S(1)}, s32[32]{0:T(128)}, u32[]{:S(2)}) copy-start(s32[32]{0:T(128)} %param.9) | copy-start | bytes 388
  144.5 15.1 %all-to-all-start = ((bf16[16,2,40,128]{3,1,2,0:T(2,128)(2,1)}), bf16[16,2,40,128]{3,1,2,0:T(2,128)(2,1)S(1)}, u32[]{:S(2)}, u32[]{:S(2)}) async-start(bf16[16,2,40,128]{3,1,2,0:T(2,128)(2,1)} %bitcast.9), calls=%async_computation | async-start | bytes 655360 | tf_op jit(solution)/shard_map/all_to_all | solution.py:49
  159.7 16.1 %copy-start.1 = (bf16[640,256]{1,0:T(8,128)(2,1)S(1)}, bf16[640,256]{1,0:T(8,128)(2,1)}, u32[]{:S(2)}) copy-start(bf16[640,256]{1,0:T(8,128)(2,1)} %param.8) | copy-start | bytes 983044
  159.7 16.1 %copy-start.2 = (f32[640]{0:T(1024)S(1)}, f32[640]{0:T(1024)}, u32[]{:S(2)}) copy-start(f32[640]{0:T(1024)} %param.12) | copy-start | bytes 7684
  161.2 14.3 %all-to-all-start.1 = ((bf16[16,2,40,128]{3,2,1,0:T(8,128)(2,1)}), bf16[16,2,40,128]{3,2,1,0:T(8,128)(2,1)S(1)}, u32[]{:S(2)}, u32[]{:S(2)}) async-start(bf16[16,2,40,128]{3,2,1,0:T(8,128)(2,1)} %broadcast_select_fusion.1), calls=%async_computation.1 | async-start | bytes 655360 | tf_op jit(solution)/shard_map/all_to_all | solution.py:51
Sparse Core Ops, SparseCore 0:
  8.9 13.2 all-gather.4
  24.9 99.5 all-gather.2
where the time goes:
time: 185 us; the launch traced here: 184 us
  waiting for transfers between devices  131 us (71%)
  matrix products  16.5 us (9%)
  between operations  13.5 us (7%)
  local copies, waits for them, and re-layouts  8.64 us (5%)
  starting transfers between devices  7.39 us (4%)
  other arithmetic  6.53 us (4%)
    all_gather x1, waiting for transfers between devices, local(): piece_in = lax.all_gather(amplitudes, 'vcol', axis=1, tiled=True)  96.8 us
    dot_general x10, matrix products, one_block(): return jnp.dot(left_rows, masked, preferred_element_type=jnp.float32)  15.1 us
    all_to_all x1, waiting for transfers between devices, local(): lax.all_to_all(parts, 'vcol', 0, 0, tiled=True)  11.2 us
    all_gather x1, waiting for transfers between devices, gather_rows(): return lax.all_gather(panel, 'pair', axis=0, tiled=True)  10.7 us
    all_to_all x1, waiting for transfers between devices, local(): back = lax.all_to_all(by_slot, 'vcol', 0, 0, tiled=True)  10.4 us
    all_to_all x1, starting transfers between devices, local(): lax.all_to_all(parts, 'vcol', 0, 0, tiled=True)  3.8 us
  transfers between devices with their start and end apart: 4, of which 4 were waited for; matrix products, arithmetic and copies ran while one was open for 5% of the time, Pallas kernels for 0%

commit v1 on v0

--- a/solution.py
+++ b/solution.py
@@ -6,6 +6,28 @@
 TILE = 128
 PBLK = 64
 KT_DEV = 2
+
+
+def in_blocks(value, dim, devices):
+    before, after = (value.shape[:dim], value.shape[dim + 1 :])
+    return jnp.moveaxis(value.reshape(*before, devices, -1, *after), dim, 0)
+
+
+def joined_along(tiles, dim):
+    tiles = jnp.moveaxis(tiles, 0, dim)
+    shape = tiles.shape
+    return tiles.reshape(*shape[:dim], shape[dim] * shape[dim + 1], *shape[dim + 2 :])
+
+
+def exchange_in_pairs(x, axis, split_dim, concat_dim):
+    length, position = (lax.axis_size(axis), lax.axis_index(axis))
+    blocks = in_blocks(x, split_dim, length)
+    finished = [blocks[position]]
+    for step in range(1, length):
+        sent = blocks[position ^ step]
+        finished.append(lax.ppermute(sent, axis, [(i, i ^ step) for i in range(length)]))
+    blocks = jnp.stack(finished)[position ^ jnp.arange(length)]
+    return joined_along(blocks, concat_dim)
 
 
 def one_hot(indices, length):
@@ -48,7 +70,7 @@
     parts = ladder_local.reshape(ranks, rows, KT_DEV, TILE).transpose(0, 2, 1, 3)
     spread = lax.all_to_all(parts, "vcol", 0, 0, tiled=True).reshape(tile_count, rows, TILE)
     by_slot = jnp.take(spread, tile_owner, axis=0).reshape(ranks, KT_DEV, rows, TILE)
-    back = lax.all_to_all(by_slot, "vcol", 0, 0, tiled=True)
+    back = exchange_in_pairs(by_slot, "vcol", 0, 0)
     ladder_owned = back.transpose(0, 2, 1, 3).reshape(pair_local, width).astype(jnp.float32)
     virt_owned = jnp.dot(
         one_hot(owned_tiles, tile_count),

time: 185 us -> 201 us (1.086)
  starting transfers between devices: 7.39 us -> 30.9 us
  waiting for transfers between devices: 131 us -> 124 us
    ppermute x0 -> x15, starting transfers between devices: none -> 27.1 us  [exchange_in_pairs(): lax.ppermute(sent, axis, [(i, i ^ step) for i in range(length)])]
    all_to_all x1 -> x0, waiting for transfers between devices: 10.4 us -> none  [local(): back = lax.all_to_all(by_slot, 'vcol', 0, 0, tiled=True)]
    ppermute x0 -> x15, waiting for transfers between devices: none -> 3.82 us  [exchange_in_pairs(): lax.ppermute(sent, axis, [(i, i ^ step) for i in range(length)])]
    all_to_all x1 -> x0, starting transfers between devices: 3.54 us -> none  [local(): back = lax.all_to_all(by_slot, 'vcol', 0, 0, tiled=True)]
  transfers between devices with their start and end apart: 4 -> 18, of which waited for: 4 -> 5; matrix products, arithmetic and copies ran while one was open for 5% -> 5% of each run, Pallas kernels for 0% -> 0%
where the time goes in v1:
time: 201 us; the launch traced here: 200 us
  waiting for transfers between devices  124 us (62%)
  starting transfers between devices  30.9 us (15%)
  matrix products  16.5 us (8%)
  between operations  13.7 us (7%)
  local copies, waits for them, and re-layouts  9.51 us (5%)
  other arithmetic  5.82 us (3%)
    all_gather x1, waiting for transfers between devices, local(): piece_in = lax.all_gather(amplitudes, 'vcol', axis=1, tiled=True)  96.8 us
    ppermute x15, starting transfers between devices, exchange_in_pairs(): lax.ppermute(sent, axis, [(i, i ^ step) for i in range(length)])  27.1 us
    dot_general x10, matrix products, one_block(): return jnp.dot(left_rows, masked, preferred_element_type=jnp.float32)  15.1 us
    all_to_all x1, waiting for transfers between devices, local(): lax.all_to_all(parts, 'vcol', 0, 0, tiled=True)  10.8 us
    all_gather x1, waiting for transfers between devices, gather_rows(): return lax.all_gather(panel, 'pair', axis=0, tiled=True)  10.7 us
  transfers between devices with their start and end apart: 18, of which 5 were waited for; matrix products, arithmetic and copies ran while one was open for 5% of the time, Pallas kernels for 0%

profile of v1, /device:TPU:0, one launch (start us, length us, event | category | flops | bytes accessed | tf_op | source)
XLA Modules:
  0.0 200.5 jit_solution(15925326912701044223)
XLA Ops:
  6.5 0.7 all-gather.5.cloned.1.call-update
  7.3 0.7 all-gather.3.cloned.1.call-update
  8.0 1.2 convolution_bitcast_fusion.1
  9.2 0.1 copy.12
  9.3 0.7 compare_select_fusion.1
  10.0 0.6 gather_fusion
  10.6 0.7 compare_and_fusion
  11.3 0.1 fusion.8
  11.5 10.7 %all-gather.5.cloned.1.call-done = bf16[4096,256]{1,0:T(8,128)(2,1)} async-done(((bf16[2048,256]{1,0:T(8,128)(2,1)}), bf16[4096,256]{1,0:T(8,128)(2,1)}) %all-gather.5.cloned.1.call-update) | async-done | bytes 2097168 | tf_op jit(solution)/shard_map/all_gather | solution.py:38
  22.2 3.7 %gather_fusion.1 = bf16[32,128,256]{2,1,0:T(8,128)(2,1)} fusion(bf16[32,128,256]{2,1,0:T(8,128)(2,1)} %bitcast.119, s32[1024]{0:T(1024)S(1)} %pad_clamp_fusion.1), kind=kCustom, calls=%fused_computation.1 | custom fusion | bytes 4194432 | tf_op jit(solution)/shard_map/jit(_take)/gather | solution.py:54
  25.9 1.8 broadcast_select_fusion
  27.7 96.8 %all-gather.3.cloned.1.call-done = bf16[640,4096]{1,0:T(8,128)(2,1)} async-done(((bf16[640,256]{1,0:T(8,128)(2,1)}), bf16[640,4096]{1,0:T(8,128)(2,1)}) %all-gather.3.cloned.1.call-update) | async-done | bytes 5242896 | tf_op jit(solution)/shard_map/all_gather | solution.py:55
  124.5 19.2 %while.10 = (s32[]{:T(128)}, bf16[10,64,256]{2,1,0:T(8,128)(2,1)S(1)}, bf16[10,64,4096]{2,1,0:T(8,128)(2,1)}, bf16[10,32,2]{1,2,0:T(2,128)(2,1)S(1)}, bf16[32,128,256]{2,1,0:T(8,128)(2,1)S(1)}, /*index=5*/s32[]{:T(128)}) while((s32[]{:T(128)}, bf16[10,64,256]{2,1,0:T(8,128)(2,1)S(1)}, bf16[10,64,4096]{2,1,0:T(8,128)(2,1)}, ...), condition=%wide.region_1.2_spmd, body=%wide.region_0.1_spmd.sunk | while | flops 135266304 | bytes 6948561 | solution.py:66
  124.5 0.1 copy.23
  124.7 0.1 broadcast_multiply_fusion.2
  124.9 1.5 fusion.25
  126.4 0.1 copy.23
  126.7 0.1 broadcast_multiply_fusion.2
  126.8 1.5 fusion.25
  128.4 0.1 copy.23
  128.6 0.1 broadcast_multiply_fusion.2
  128.7 1.5 fusion.25
  130.5 0.1 broadcast_multiply_fusion.2
  130.7 1.5 fusion.25
  132.2 0.1 copy.23
  132.4 0.1 broadcast_multiply_fusion.2
  132.6 1.5 fusion.25
  134.4 0.1 broadcast_multiply_fusion.2
  134.5 1.5 fusion.25
  136.3 0.1 broadcast_multiply_fusion.2
  136.4 1.5 fusion.25
  138.2 0.1 broadcast_multiply_fusion.2
  138.4 1.5 fusion.25
  140.1 0.1 broadcast_multiply_fusion.2
  140.3 1.5 fusion.25
  142.0 0.1 broadcast_multiply_fusion.2
  142.2 1.5 fusion.25
  143.7 0.8 convert_element_type.36
  144.5 3.8 %all-to-all-start = ((bf16[16,2,40,128]{3,1,2,0:T(2,128)(2,1)}), bf16[16,2,40,128]{3,1,2,0:T(2,128)(2,1)S(1)}, u32[]{:S(2)}, u32[]{:S(2)}) async-start(bf16[16,2,40,128]{3,1,2,0:T(2,128)(2,1)} %bitcast.9), calls=%async_computation | async-start | bytes 655360 | tf_op jit(solution)/shard_map/all_to_all | solution.py:71
  148.6 0.2 convolution_bitcast_fusion.2
  148.8 10.8 %all-to-all-done = bf16[16,2,40,128]{3,1,2,0:T(2,128)(2,1)S(1)} async-done(((bf16[16,2,40,128]{3,1,2,0:T(2,128)(2,1)}), bf16[16,2,40,128]{3,1,2,0:T(2,128)(2,1)S(1)}, u32[]{:S(2)}, u32[]{:S(2)}) %all-to-all-start) | async-done | bytes 327712 | tf_op jit(solution)/shard_map/all_to_all | solution.py:71
  159.7 0.6 gather_fusion.2
  160.3 0.1 broadcast_select_fusion.1
  160.5 0.1 dynamic-slice_bitcast_fusion
  160.6 0.6 collective-permute-start
  161.2 0.8 collective-permute-start.1
  162.0 2.1 %collective-permute-start.2 = (bf16[1,2,40,128]{3,2,1,0:T(8,128)(2,1)S(1)}, bf16[1,2,40,128]{3,2,1,0:T(8,128)(2,1)S(1)}, u32[]{:S(2)}, u32[]{:S(2)}) collective-permute-start(bf16[1,2,40,128]{3,2,1,0:T(8,128)(2,1)S(1)} %get-tuple-element.65), channel_id=1, source_target_pairs={{0,3},{1,2},{2,1},{3,0},{4,7},{5,6},{6,5},{7,4},{8,11},{9,10},{10,... | collective-permute-start | bytes 61448 | tf_op jit(solution)/shard_map/ppermute | solution.py:28
  164.2 1.0 collective-permute-start.3
  165.2 1.0 collective-permute-start.4
  166.2 1.2 collective-permute-start.5
  167.4 2.7 %collective-permute-start.6 = (bf16[1,2,40,128]{3,2,1,0:T(8,128)(2,1)S(1)}, bf16[1,2,40,128]{3,2,1,0:T(8,128)(2,1)S(1)}, u32[]{:S(2)}, u32[]{:S(2)}) collective-permute-start(bf16[1,2,40,128]{3,2,1,0:T(8,128)(2,1)S(1)} %get-tuple-element.61), channel_id=1, source_target_pairs={{0,7},{1,6},{2,5},{3,4},{4,3},{5,2},{6,1},{7,0},{8,15},{9,14},{10,... | collective-permute-start | bytes 61448 | tf_op jit(solution)/shard_map/ppermute | solution.py:28
  170.1 0.4 collective-permute-start.7
  170.5 2.7 %collective-permute-start.8 = (bf16[1,2,40,128]{3,2,1,0:T(8,128)(2,1)S(1)}, bf16[1,2,40,128]{3,2,1,0:T(8,128)(2,1)S(1)}, u32[]{:S(2)}, u32[]{:S(2)}) collective-permute-start(bf16[1,2,40,128]{3,2,1,0:T(8,128)(2,1)S(1)} %get-tuple-element.59), channel_id=1, source_target_pairs={{0,9},{1,8},{2,11},{3,10},{4,13},{5,12},{6,15},{7,14},{8,1},{9,0},... | collective-permute-start | bytes 61448 | tf_op jit(solution)/shard_map/ppermute | solution.py:28
  173.2 0.9 collective-permute-start.9
  174.1 4.0 %collective-permute-start.10 = (bf16[1,2,40,128]{3,2,1,0:T(8,128)(2,1)S(1)}, bf16[1,2,40,128]{3,2,1,0:T(8,128)(2,1)S(1)}, u32[]{:S(2)}, u32[]{:S(2)}) collective-permute-start(bf16[1,2,40,128]{3,2,1,0:T(8,128)(2,1)S(1)} %get-tuple-element.57), channel_id=1, source_target_pairs={{0,11},{1,10},{2,9},{3,8},{4,15},{5,14},{6,13},{7,12},{8,3},{9,2},... | collective-permute-start | bytes 61448 | tf_op jit(solution)/shard_map/ppermute | solution.py:28
  178.1 1.7 collective-permute-start.11
  179.8 2.2 %collective-permute-start.12 = (bf16[1,2,40,128]{3,2,1,0:T(8,128)(2,1)S(1)}, bf16[1,2,40,128]{3,2,1,0:T(8,128)(2,1)S(1)}, u32[]{:S(2)}, u32[]{:S(2)}) collective-permute-start(bf16[1,2,40,128]{3,2,1,0:T(8,128)(2,1)S(1)} %get-tuple-element.55), channel_id=1, source_target_pairs={{0,13},{1,12},{2,15},{3,14},{4,9},{5,8},{6,11},{7,10},{8,5},{9,4},... | collective-permute-start | bytes 61448 | tf_op jit(solution)/shard_map/ppermute | solution.py:28
  182.0 2.2 %collective-permute-start.13 = (bf16[1,2,40,128]{3,2,1,0:T(8,128)(2,1)S(1)}, bf16[1,2,40,128]{3,2,1,0:T(8,128)(2,1)S(1)}, u32[]{:S(2)}, u32[]{:S(2)}) collective-permute-start(bf16[1,2,40,128]{3,2,1,0:T(8,128)(2,1)S(1)} %get-tuple-element.54), channel_id=1, source_target_pairs={{0,14},{1,15},{2,12},{3,13},{4,10},{5,11},{6,8},{7,9},{8,6},{9,7},... | collective-permute-start | bytes 61448 | tf_op jit(solution)/shard_map/ppermute | solution.py:28
  184.2 3.6 %collective-permute-start.14 = (bf16[1,2,40,128]{3,2,1,0:T(8,128)(2,1)S(1)}, bf16[1,2,40,128]{3,2,1,0:T(8,128)(2,1)S(1)}, u32[]{:S(2)}, u32[]{:S(2)}) collective-permute-start(bf16[1,2,40,128]{3,2,1,0:T(8,128)(2,1)S(1)} %get-tuple-element.53), channel_id=1, source_target_pairs={{0,15},{1,14},{2,13},{3,12},{4,11},{5,10},{6,9},{7,8},{8,7},{9,6},... | collective-permute-start | bytes 61448 | tf_op jit(solution)/shard_map/ppermute | solution.py:28
  187.9 0.7 collective-permute-done.13
  188.6 3.1 %collective-permute-done.14 = bf16[1,2,40,128]{3,2,1,0:T(8,128)(2,1)S(1)} collective-permute-done((bf16[1,2,40,128]{3,2,1,0:T(8,128)(2,1)S(1)}, bf16[1,2,40,128]{3,2,1,0:T(8,128)(2,1)S(1)}, u32[]{:S(2)}, u32[]{:S(2)}) %collective-permute-start.14) | collective-permute-done | bytes 20512 | tf_op jit(solution)/shard_map/ppermute | solution.py:28
  191.7 0.6 gather_fusion.3
  192.4 0.3 copy.15
  192.7 0.9 fusion.5
  (84 shorter events, 2.3 us)
Async XLA Ops:
  6.5 142.1 %copy-start = (f32[4096]{0:T(1024)S(1)}, f32[4096]{0:T(1024)}, u32[]{:S(2)}) copy-start(f32[4096]{0:T(1024)} %param.13) | copy-start | bytes 49156
  6.5 15.7 %all-gather.5.cloned.1.call-start = ((), (), s32[]{:S(2)}) async-start(), calls=%async_computation.2 | async-start | bytes 3145728 | tf_op jit(solution)/shard_map/all_gather | solution.py:38
  7.3 117.2 %all-gather.3.cloned.1.call-start = ((), (), s32[]{:S(2)}) async-start(), calls=%async_computation.1 | async-start | bytes 5570560 | tf_op jit(solution)/shard_map/all_gather | solution.py:55
  124.5 24.0 %copy-start.3 = (s32[32]{0:T(128)S(1)}, s32[32]{0:T(128)}, u32[]{:S(2)}) copy-start(s32[32]{0:T(128)} %param.9) | copy-start | bytes 388
  144.5 15.1 %all-to-all-start = ((bf16[16,2,40,128]{3,1,2,0:T(2,128)(2,1)}), bf16[16,2,40,128]{3,1,2,0:T(2,128)(2,1)S(1)}, u32[]{:S(2)}, u32[]{:S(2)}) async-start(bf16[16,2,40,128]{3,1,2,0:T(2,128)(2,1)} %bitcast.9), calls=%async_computation | async-start | bytes 655360 | tf_op jit(solution)/shard_map/all_to_all | solution.py:71
  160.5 32.3 %copy-start.1 = (bf16[640,256]{1,0:T(8,128)(2,1)S(1)}, bf16[640,256]{1,0:T(8,128)(2,1)}, u32[]{:S(2)}) copy-start(bf16[640,256]{1,0:T(8,128)(2,1)} %param.8) | copy-start | bytes 983044
  160.5 32.3 %copy-start.2 = (f32[640]{0:T(1024)S(1)}, f32[640]{0:T(1024)}, u32[]{:S(2)}) copy-start(f32[640]{0:T(1024)} %param.12) | copy-start | bytes 7684
  160.6 5.6 %collective-permute-start = (bf16[1,2,40,128]{3,2,1,0:T(8,128)(2,1)S(1)}, bf16[1,2,40,128]{3,2,1,0:T(8,128)(2,1)S(1)}, u32[]{:S(2)}, u32[]{:S(2)}) collective-permute-start(bf16[1,2,40,128]{3,2,1,0:T(8,128)(2,1)S(1)} %get-tuple-element.67), channel_id=1, source_target_pairs={{0,1},{1,0},{2,3},{3,2},{4,5},{5,4},{6,7},{7,6},{8,9},{9,8},{10,11... | collective-permute-start | bytes 61448 | tf_op jit(solution)/shard_map/ppermute | solution.py:28
  161.2 6.2 %collective-permute-start.1 = (bf16[1,2,40,128]{3,2,1,0:T(8,128)(2,1)S(1)}, bf16[1,2,40,128]{3,2,1,0:T(8,128)(2,1)S(1)}, u32[]{:S(2)}, u32[]{:S(2)}) collective-permute-start(bf16[1,2,40,128]{3,2,1,0:T(8,128)(2,1)S(1)} %get-tuple-element.66), channel_id=1, source_target_pairs={{0,2},{1,3},{2,0},{3,1},{4,6},{5,7},{6,4},{7,5},{8,10},{9,11},{10,... | collective-permute-start | bytes 61448 | tf_op jit(solution)/shard_map/ppermute | solution.py:28
  162.0 8.1 %collective-permute-start.2 = (bf16[1,2,40,128]{3,2,1,0:T(8,128)(2,1)S(1)}, bf16[1,2,40,128]{3,2,1,0:T(8,128)(2,1)S(1)}, u32[]{:S(2)}, u32[]{:S(2)}) collective-permute-start(bf16[1,2,40,128]{3,2,1,0:T(8,128)(2,1)S(1)} %get-tuple-element.65), channel_id=1, source_target_pairs={{0,3},{1,2},{2,1},{3,0},{4,7},{5,6},{6,5},{7,4},{8,11},{9,10},{10,... | collective-permute-start | bytes 61448 | tf_op jit(solution)/shard_map/ppermute | solution.py:28
  164.2 6.3 %collective-permute-start.3 = (bf16[1,2,40,128]{3,2,1,0:T(8,128)(2,1)S(1)}, bf16[1,2,40,128]{3,2,1,0:T(8,128)(2,1)S(1)}, u32[]{:S(2)}, u32[]{:S(2)}) collective-permute-start(bf16[1,2,40,128]{3,2,1,0:T(8,128)(2,1)S(1)} %get-tuple-element.64), channel_id=1, source_target_pairs={{0,4},{1,5},{2,6},{3,7},{4,0},{5,1},{6,2},{7,3},{8,12},{9,13},{10,... | collective-permute-start | bytes 61448 | tf_op jit(solution)/shard_map/ppermute | solution.py:28
  165.2 8.0 %collective-permute-start.4 = (bf16[1,2,40,128]{3,2,1,0:T(8,128)(2,1)S(1)}, bf16[1,2,40,128]{3,2,1,0:T(8,128)(2,1)S(1)}, u32[]{:S(2)}, u32[]{:S(2)}) collective-permute-start(bf16[1,2,40,128]{3,2,1,0:T(8,128)(2,1)S(1)} %get-tuple-element.63), channel_id=1, source_target_pairs={{0,5},{1,4},{2,7},{3,6},{4,1},{5,0},{6,3},{7,2},{8,13},{9,12},{10,... | collective-permute-start | bytes 61448 | tf_op jit(solution)/shard_map/ppermute | solution.py:28
  166.2 7.9 %collective-permute-start.5 = (bf16[1,2,40,128]{3,2,1,0:T(8,128)(2,1)S(1)}, bf16[1,2,40,128]{3,2,1,0:T(8,128)(2,1)S(1)}, u32[]{:S(2)}, u32[]{:S(2)}) collective-permute-start(bf16[1,2,40,128]{3,2,1,0:T(8,128)(2,1)S(1)} %get-tuple-element.62), channel_id=1, source_target_pairs={{0,6},{1,7},{2,4},{3,5},{4,2},{5,3},{6,0},{7,1},{8,14},{9,15},{10,... | collective-permute-start | bytes 61448 | tf_op jit(solution)/shard_map/ppermute | solution.py:28
  167.4 10.6 %collective-permute-start.6 = (bf16[1,2,40,128]{3,2,1,0:T(8,128)(2,1)S(1)}, bf16[1,2,40,128]{3,2,1,0:T(8,128)(2,1)S(1)}, u32[]{:S(2)}, u32[]{:S(2)}) collective-permute-start(bf16[1,2,40,128]{3,2,1,0:T(8,128)(2,1)S(1)} %get-tuple-element.61), channel_id=1, source_target_pairs={{0,7},{1,6},{2,5},{3,4},{4,3},{5,2},{6,1},{7,0},{8,15},{9,14},{10,... | collective-permute-start | bytes 61448 | tf_op jit(solution)/shard_map/ppermute | solution.py:28
  170.1 9.7 %collective-permute-start.7 = (bf16[1,2,40,128]{3,2,1,0:T(8,128)(2,1)S(1)}, bf16[1,2,40,128]{3,2,1,0:T(8,128)(2,1)S(1)}, u32[]{:S(2)}, u32[]{:S(2)}) collective-permute-start(bf16[1,2,40,128]{3,2,1,0:T(8,128)(2,1)S(1)} %get-tuple-element.60), channel_id=1, source_target_pairs={{0,8},{1,9},{2,10},{3,11},{4,12},{5,13},{6,14},{7,15},{8,0},{9,1},... | collective-permute-start | bytes 61448 | tf_op jit(solution)/shard_map/ppermute | solution.py:28
  170.5 11.5 %collective-permute-start.8 = (bf16[1,2,40,128]{3,2,1,0:T(8,128)(2,1)S(1)}, bf16[1,2,40,128]{3,2,1,0:T(8,128)(2,1)S(1)}, u32[]{:S(2)}, u32[]{:S(2)}) collective-permute-start(bf16[1,2,40,128]{3,2,1,0:T(8,128)(2,1)S(1)} %get-tuple-element.59), channel_id=1, source_target_pairs={{0,9},{1,8},{2,11},{3,10},{4,13},{5,12},{6,15},{7,14},{8,1},{9,0},... | collective-permute-start | bytes 61448 | tf_op jit(solution)/shard_map/ppermute | solution.py:28
  173.2 11.0 %collective-permute-start.9 = (bf16[1,2,40,128]{3,2,1,0:T(8,128)(2,1)S(1)}, bf16[1,2,40,128]{3,2,1,0:T(8,128)(2,1)S(1)}, u32[]{:S(2)}, u32[]{:S(2)}) collective-permute-start(bf16[1,2,40,128]{3,2,1,0:T(8,128)(2,1)S(1)} %get-tuple-element.58), channel_id=1, source_target_pairs={{0,10},{1,11},{2,8},{3,9},{4,14},{5,15},{6,12},{7,13},{8,2},{9,3},... | collective-permute-start | bytes 61448 | tf_op jit(solution)/shard_map/ppermute | solution.py:28
  174.1 13.7 %collective-permute-start.10 = (bf16[1,2,40,128]{3,2,1,0:T(8,128)(2,1)S(1)}, bf16[1,2,40,128]{3,2,1,0:T(8,128)(2,1)S(1)}, u32[]{:S(2)}, u32[]{:S(2)}) collective-permute-start(bf16[1,2,40,128]{3,2,1,0:T(8,128)(2,1)S(1)} %get-tuple-element.57), channel_id=1, source_target_pairs={{0,11},{1,10},{2,9},{3,8},{4,15},{5,14},{6,13},{7,12},{8,3},{9,2},... | collective-permute-start | bytes 61448 | tf_op jit(solution)/shard_map/ppermute | solution.py:28
  178.1 9.8 %collective-permute-start.11 = (bf16[1,2,40,128]{3,2,1,0:T(8,128)(2,1)S(1)}, bf16[1,2,40,128]{3,2,1,0:T(8,128)(2,1)S(1)}, u32[]{:S(2)}, u32[]{:S(2)}) collective-permute-start(bf16[1,2,40,128]{3,2,1,0:T(8,128)(2,1)S(1)} %get-tuple-element.56), channel_id=1, source_target_pairs={{0,12},{1,13},{2,14},{3,15},{4,8},{5,9},{6,10},{7,11},{8,4},{9,5},... | collective-permute-start | bytes 61448 | tf_op jit(solution)/shard_map/ppermute | solution.py:28
  179.8 8.0 %collective-permute-start.12 = (bf16[1,2,40,128]{3,2,1,0:T(8,128)(2,1)S(1)}, bf16[1,2,40,128]{3,2,1,0:T(8,128)(2,1)S(1)}, u32[]{:S(2)}, u32[]{:S(2)}) collective-permute-start(bf16[1,2,40,128]{3,2,1,0:T(8,128)(2,1)S(1)} %get-tuple-element.55), channel_id=1, source_target_pairs={{0,13},{1,12},{2,15},{3,14},{4,9},{5,8},{6,11},{7,10},{8,5},{9,4},... | collective-permute-start | bytes 61448 | tf_op jit(solution)/shard_map/ppermute | solution.py:28
  182.0 6.5 %collective-permute-start.13 = (bf16[1,2,40,128]{3,2,1,0:T(8,128)(2,1)S(1)}, bf16[1,2,40,128]{3,2,1,0:T(8,128)(2,1)S(1)}, u32[]{:S(2)}, u32[]{:S(2)}) collective-permute-start(bf16[1,2,40,128]{3,2,1,0:T(8,128)(2,1)S(1)} %get-tuple-element.54), channel_id=1, source_target_pairs={{0,14},{1,15},{2,12},{3,13},{4,10},{5,11},{6,8},{7,9},{8,6},{9,7},... | collective-permute-start | bytes 61448 | tf_op jit(solution)/shard_map/ppermute | solution.py:28
  184.2 7.4 %collective-permute-start.14 = (bf16[1,2,40,128]{3,2,1,0:T(8,128)(2,1)S(1)}, bf16[1,2,40,128]{3,2,1,0:T(8,128)(2,1)S(1)}, u32[]{:S(2)}, u32[]{:S(2)}) collective-permute-start(bf16[1,2,40,128]{3,2,1,0:T(8,128)(2,1)S(1)} %get-tuple-element.53), channel_id=1, source_target_pairs={{0,15},{1,14},{2,13},{3,12},{4,11},{5,10},{6,9},{7,8},{8,7},{9,6},... | collective-permute-start | bytes 61448 | tf_op jit(solution)/shard_map/ppermute | solution.py:28
Sparse Core Ops, SparseCore 0:
  8.9 13.2 all-gather.4
  24.9 99.5 all-gather.2
